TPU v7x, 32 devices: a whole 2x2x4 slice. The times are simulated.
32 devices in a mesh: row: 4 (over y, x), col: 8 (over z, core).
Axes of the slice: x: 2, y: 2, z: 4, core: 2. Of those that a mesh axis runs over, the one named last changes fastest.
Arguments:
- noise: float32 [2048, 3072], P('row', 'col'), may hold values from -30 to 30
- images: float32 [6144, 3072], P('col', 'row'), may hold values from -6 to 6
- time_index: int32 [2048], P('row'), may hold values from 0 to 999
- w_in: float32 [3072, 3072], P(None, 'col'), may hold values from -0.109375 to 0.109375
- time_gain: float32 [3072], P('col'), may hold values from -5 to 5
- w_out: float32 [3072, 3072], P('col'), may hold values from -0.109375 to 0.109375
Outputs:
- targets: float32 [2048, 3072], P('row', 'col')
- row_pot: float32 [2048], P('row')
- col_pot: float32 [6144], P('col')
- grad_in: float32 [3072, 3072], P('row', 'col')
- grad_time: float32 [3072], P('col')
- grad_out: float32 [3072, 3072], P('col', 'row')
- mse: float32 [], replicated
All inputs are finite; a program needn't handle non-finite values.
Results may differ from a plain program's by a relative error of at most 0.0003.
Values sent between devices are 32-bit elements; how exact they have to be, the bound alone decides.
A program may use at most 128 MiB of HBM per device.

v0:
```python
import jax
import jax.numpy as jnp
from jax import lax
from jax.sharding import PartitionSpec as P

ITERS = 2
TIMES = 1000
EPSILON = 0.01


def merged(array, axis, combine):
    everything = jax.tree.map(lambda part: lax.all_gather(part, axis), array)
    first = jax.tree.map(lambda part: part[0], everything)

    def hop(k, so_far):
        return combine(so_far, jax.tree.map(lambda part: part[k], everything))

    return lax.fori_loop(1, lax.axis_size(axis), hop, first)


def joined(left_pair, right_pair):
    peak = jnp.maximum(left_pair[0], right_pair[0])
    total = left_pair[1] * jnp.exp(left_pair[0] - peak) + right_pair[1] * jnp.exp(
        right_pair[0] - peak
    )
    return (peak, total)


def over_images(logits):
    local_peak = jnp.max(logits, axis=1)
    local_total = jnp.sum(jnp.exp(logits - local_peak[:, None]), axis=1)
    peak, total = merged((local_peak, local_total), "col", joined)
    return (peak, total)


def over_noise(logits):
    local_peak = jnp.max(logits, axis=0)
    local_total = jnp.sum(jnp.exp(logits - local_peak[None, :]), axis=0)
    peak, total = merged((local_peak, local_total), "row", joined)
    return (peak, total)


def body(noise, images, time_index, w_in, time_gain, w_out):
    highest = lax.Precision.HIGHEST
    full_noise = lax.all_gather(noise, "col", axis=1, tiled=True)
    full_images = lax.all_gather(images, "row", axis=1, tiled=True)
    width = full_noise.shape[1]
    noise_count = full_noise.shape[0] * lax.axis_size("row")
    image_count = full_images.shape[0] * lax.axis_size("col")
    noise_norms = jnp.sum(full_noise * full_noise, axis=1)
    image_norms = jnp.sum(full_images * full_images, axis=1)
    cross = lax.dot_general(
        full_noise,
        full_images,
        (((1,), (1,)), ((), ())),
        precision=highest,
        preferred_element_type=jnp.float32,
    )
    scaled = (noise_norms[:, None] + image_norms[None, :] - 2.0 * cross) / (width * EPSILON)
    col_pot = jnp.zeros((full_images.shape[0],), jnp.float32)
    row_pot = jnp.zeros((full_noise.shape[0],), jnp.float32)
    for iteration in range(ITERS):
        peak, total = over_images(col_pot[None, :] - scaled)
        row_pot = jnp.log(jnp.float32(image_count)) - (jnp.log(total) + peak)
        peak, total = over_noise(row_pot[:, None] - scaled)
        col_pot = jnp.log(jnp.float32(noise_count)) - (jnp.log(total) + peak)
    logits = col_pot[None, :] - scaled
    peak, total = over_images(logits)
    weights = jnp.exp(logits - (jnp.log(total) + peak)[:, None])
    partial_value = jnp.dot(
        weights, full_images, precision=highest, preferred_element_type=jnp.float32
    )
    slice_width = noise.shape[1]
    slice_start = lax.axis_index("col") * slice_width
    whole_targets = lax.psum(partial_value, "col")
    targets = lax.dynamic_slice_in_dim(whole_targets, slice_start, slice_width, 1)
    fraction = (time_index.astype(jnp.float32) + 0.5) / TIMES
    mixed = (1.0 - fraction)[:, None] * full_noise + fraction[:, None] * whole_targets
    velocity = whole_targets - full_noise
    pre = (
        jnp.dot(mixed, w_in, precision=highest, preferred_element_type=jnp.float32)
        + fraction[:, None] * time_gain[None, :]
    )
    sigma = jax.nn.sigmoid(pre)
    hidden = pre * sigma
    part_out = jnp.dot(hidden, w_out, precision=highest, preferred_element_type=jnp.float32)
    out = lax.psum(part_out, "col")
    diff = out - velocity
    squared = jnp.sum(diff * diff)
    slope = diff / jnp.sqrt(jnp.float32(noise_count))
    local_out = lax.dot_general(
        hidden,
        slope,
        (((0,), (0,)), ((), ())),
        precision=highest,
        preferred_element_type=jnp.float32,
    )
    back = lax.dot_general(
        slope,
        w_out,
        (((1,), (1,)), ((), ())),
        precision=highest,
        preferred_element_type=jnp.float32,
    )
    dpre = back * sigma * (1.0 + pre * (1.0 - sigma))
    local_in = lax.dot_general(
        mixed, dpre, (((0,), (0,)), ((), ())), precision=highest, preferred_element_type=jnp.float32
    )
    local_time = jnp.sum(fraction[:, None] * dpre, axis=0)
    grad_in, grad_out = (
        lax.psum_scatter(local_in, "row", scatter_dimension=0, tiled=True),
        lax.psum_scatter(local_out, "row", scatter_dimension=1, tiled=True),
    )
    grad_time, squared_all = lax.psum((local_time, squared), "row")
    mse = squared_all / (noise_count * width)
    return (targets, row_pot, col_pot, grad_in, grad_time, grad_out, mse)


def solution(mesh):
    placed = (P("row", "col"), P("col", "row"), P("row"), P(None, "col"), P("col"), P("col", None))
    return jax.shard_map(
        body,
        mesh=mesh,
        in_specs=placed,
        out_specs=(
            P("row", "col"),
            P("row"),
            P("col"),
            P("row", "col"),
            P("col"),
            P("col", "row"),
            P(),
        ),
        check_vma=False,
    )
```

profile of v0, /device:TPU:0, one launch (start us, length us, event | category | flops | bytes accessed | tf_op | source)
XLA Modules:
  0.0 786.1 jit_solution(18099109052659360453)
XLA Ops:
  7.2 0.7 all-gather.23.cloned.1.call-update
  7.9 0.7 all-gather.25.cloned.1.call-update
  8.7 68.3 %all-gather.23.cloned.1.call-done = f32[512,3072]{1,0:T(8,128)} async-done(((f32[512,384]{1,0:T(8,128)}), f32[512,3072]{1,0:T(8,128)}) %all-gather.23.cloned.1.call-update) | async-done | bytes 6291472 | tf_op jit(solution)/shard_map/all_gather | solution.py:45
  77.0 3.3 multiply_reduce_fusion.2
  80.3 93.5 %all-gather.25.cloned.1.call-done = f32[768,3072]{1,0:T(8,128)} async-done(((f32[768,768]{1,0:T(8,128)}), f32[768,3072]{1,0:T(8,128)}) %all-gather.25.cloned.1.call-update) | async-done | bytes 9437200 | tf_op jit(solution)/shard_map/all_gather | solution.py:46
  173.8 4.5 multiply_reduce_fusion
  178.3 1.0 copy-done
  179.2 18.3 %subtract_reduce_fusion.3 = (f32[512]{0:T(512)S(1)}, f32[512,768]{1,0:T(8,128)S(1)}) fusion(f32[512,3072]{1,0:T(8,128)S(1)} %copy-done, f32[768,3072]{1,0:T(8,128)} %all-gather.25.cloned.1.call-done, f32[768]{0:T(1024)S(1)} %multiply_reduce_fusion, f32[512]{0:T(512)S(1)} %multiply_reduce_fusion.2), kind=kOutput, calls=%fused_computation.38 | convolution fusion | flops 14497873920 | bytes 17308672 | tf_op jit(solution)/shard_map/dot_general | solution.py:52
  197.5 0.4 exponential_reduce_fusion.4
  197.9 12.8 %all-gather.11 = f32[8,1,512]{2,1,0:T(1,128)S(1)} all-gather(f32[1,1,512]{2,1,0:T(1,128)S(1)} %bitcast.95), channel_id=3, replica_groups=mesh['row'=4,'col'=8] {'col'}, dimensions={0}, use_global_device_ids=true | all-gather | bytes 18432 | tf_op jit(solution)/shard_map/all_gather | solution.py:12
  210.8 12.8 %all-gather.10 = f32[8,1,512]{2,1,0:T(1,128)S(1)} all-gather(f32[1,1,512]{2,1,0:T(1,128)S(1)} %bitcast.93), channel_id=2, replica_groups=mesh['row'=4,'col'=8] {'col'}, dimensions={0}, use_global_device_ids=true | all-gather | bytes 18432 | tf_op jit(solution)/shard_map/all_gather | solution.py:12
  223.5 0.4 while.85
  224.1 0.3 exponential_reduce_fusion.3
  224.5 8.1 %all-gather.13 = f32[4,1,768]{2,1,0:T(1,128)S(1)} all-gather(f32[1,1,768]{2,1,0:T(1,128)S(1)} %reshape.65), channel_id=5, replica_groups=mesh['row'=4,'col'=8] {'row'}, dimensions={0}, use_global_device_ids=true | all-gather | bytes 15360 | tf_op jit(solution)/shard_map/all_gather | solution.py:12
  232.6 7.2 all-gather.12
  239.9 0.2 while.86
  240.3 0.4 exponential_reduce_fusion.2
  240.7 12.8 %all-gather.15 = f32[8,1,512]{2,1,0:T(1,128)S(1)} all-gather(f32[1,1,512]{2,1,0:T(1,128)S(1)} %bitcast.94), channel_id=7, replica_groups=mesh['row'=4,'col'=8] {'col'}, dimensions={0}, use_global_device_ids=true | all-gather | bytes 18432 | tf_op jit(solution)/shard_map/all_gather | solution.py:12
  253.5 12.8 %all-gather.14 = f32[8,1,512]{2,1,0:T(1,128)S(1)} all-gather(f32[1,1,512]{2,1,0:T(1,128)S(1)} %bitcast.91), channel_id=6, replica_groups=mesh['row'=4,'col'=8] {'col'}, dimensions={0}, use_global_device_ids=true | all-gather | bytes 18432 | tf_op jit(solution)/shard_map/all_gather | solution.py:12
  266.3 0.4 while.87
  266.9 0.3 exponential_reduce_fusion.1
  267.2 8.1 %all-gather.17 = f32[4,1,768]{2,1,0:T(1,128)S(1)} all-gather(f32[1,1,768]{2,1,0:T(1,128)S(1)} %reshape.73), channel_id=9, replica_groups=mesh['row'=4,'col'=8] {'row'}, dimensions={0}, use_global_device_ids=true | all-gather | bytes 15360 | tf_op jit(solution)/shard_map/all_gather | solution.py:12
  275.4 18.3 %all-gather.16 = f32[4,1,768]{2,1,0:T(1,128)S(1)} all-gather(f32[1,1,768]{2,1,0:T(1,128)S(1)} %reshape.71), channel_id=8, replica_groups=mesh['row'=4,'col'=8] {'row'}, dimensions={0}, use_global_device_ids=true | all-gather | bytes 15360 | tf_op jit(solution)/shard_map/all_gather | solution.py:12
  293.7 0.2 while.88
  293.9 0.2 subtract_reduce_fusion.4
  294.1 0.4 exponential_reduce_fusion
  294.6 12.8 %all-gather.19 = f32[8,1,512]{2,1,0:T(1,128)S(1)} all-gather(f32[1,1,512]{2,1,0:T(1,128)S(1)} %bitcast.96), channel_id=11, replica_groups=mesh['row'=4,'col'=8] {'col'}, dimensions={0}, use_global_device_ids=true | all-gather | bytes 18432 | tf_op jit(solution)/shard_map/all_gather | solution.py:12
  307.3 12.8 %all-gather.18 = f32[8,1,512]{2,1,0:T(1,128)S(1)} all-gather(f32[1,1,512]{2,1,0:T(1,128)S(1)} %bitcast.92), channel_id=10, replica_groups=mesh['row'=4,'col'=8] {'col'}, dimensions={0}, use_global_device_ids=true | all-gather | bytes 18432 | tf_op jit(solution)/shard_map/all_gather | solution.py:12
  320.1 0.4 while.89
  320.5 19.3 %fusion.6 = f32[512,3072]{1,0:T(8,128)} fusion(f32[768,3072]{1,0:T(8,128)} %all-gather.25.cloned.1.call-done, f32[512,768]{1,0:T(8,128)S(1)} %get-tuple-element.759, f32[512]{0:T(512)S(1)} %log_add_fusion, f32[768]{0:T(1024)S(1)} %add_subtract_fusion), kind=kOutput, calls=%fused_computation.26 | convolution fusion | flops 14496301056 | bytes 17306624 | tf_op jit(solution)/shard_map/dot_general | solution.py:70
  339.9 0.6 copy-done.6
  340.4 133.1 %all-reduce.4.cloned.1.call-done = f32[512,3072]{1,0:T(8,128)} async-done(((f32[512,3072]{1,0:T(8,128)}), f32[512,3072]{1,0:T(8,128)}) %all-reduce.4.cloned.1.call-update) | async-done | bytes 6291472 | tf_op jit(solution)/shard_map/psum | solution.py:75
  473.6 14.6 %convolution_add_fusion = f32[512,384]{1,0:T(8,128)S(1)} fusion(f32[3072,384]{1,0:T(8,128)} %param.19, f32[384]{0:T(512)S(1)} %copy-done.7, f32[512]{0:T(512)S(1)} %get-tuple-element.757, f32[512,3072]{1,0:T(8,128)} %all-reduce.4.cloned.1.call-done, f32[512,3072]{1,0:T(8,128)} %all-gather.23.cloned.1.call-done, f32[512]{0:T(512)S(1)} %get-tuple-element.756), kind=kOutput, calls=%fused_computation.43 | convolution fusion | flops 7252869120 | bytes 18093568 | tf_op jit(solution)/shard_map/dot_general | solution.py:81
  488.2 0.9 copy-done.2
  489.1 12.0 %fusion.20 = f32[512,3072]{1,0:T(8,128)} fusion(f32[384,3072]{1,0:T(8,128)S(1)} %bitcast.68, f32[512,384]{1,0:T(8,128)S(1)} %convolution_add_fusion), kind=kOutput, calls=%fused_computation.49 | convolution fusion | flops 7248543744 | bytes 11796480 | tf_op jit(solution)/shard_map/dot_general | solution.py:86
  501.1 0.3 reduce-scatter.5.cloned.1.call-start
  501.4 136.0 %all-reduce.6.cloned.1.call-done = f32[512,3072]{1,0:T(8,128)} async-done(((f32[512,3072]{1,0:T(8,128)}), f32[512,3072]{1,0:T(8,128)}) %all-reduce.6.cloned.1.call-update) | async-done | bytes 6291472 | tf_op jit(solution)/shard_map/psum | solution.py:87
  637.3 9.5 %multiply_reduce_fusion.1 = (f32[]{:T(128)}, f32[512,3072]{1,0:T(8,128)S(1)}) fusion(f32[512,3072]{1,0:T(8,128)} %all-reduce.6.cloned.1.call-done, f32[512,3072]{1,0:T(8,128)} %all-reduce.4.cloned.1.call-done, f32[512,3072]{1,0:T(8,128)} %all-gather.23.cloned.1.call-done), kind=kLoop, calls=%fused_computation.16 | loop fusion | flops 6291455 | bytes 25165828 | tf_op jit(solution)/shard_map/reduce_sum | solution.py:89
  646.8 2.6 copy-done.1
  649.4 10.6 %fusion = f32[384,3072]{1,0:T(8,128)} fusion(f32[512,3072]{1,0:T(8,128)S(1)} %get-tuple-element.745, f32[512,384]{1,0:T(8,128)} %copy-done.2), kind=kOutput, calls=%fused_computation.20 | convolution fusion | flops 7250116608 | bytes 11796480 | tf_op jit(solution)/shard_map/dot_general | solution.py:91
  660.1 0.3 reduce-scatter.3.cloned.1.call-start
  660.4 0.8 copy-done.3
  661.2 14.1 %multiply_reduce_fusion.3 = (f32[384]{0:T(512)S(1)}, f32[512,384]{1,0:T(8,128)S(1)}) fusion(f32[512]{0:T(512)S(1)} %get-tuple-element.757, f32[512,384]{1,0:T(8,128)S(1)} %copy-done.3, f32[384,3072]{1,0:T(8,128)} %param.21, f32[512,3072]{1,0:T(8,128)} %copy-done.1), kind=kOutput, calls=%fused_computation.44 | convolution fusion | flops 7251295744 | bytes 12586496 | tf_op jit(solution)/shard_map/dot_general | solution.py:98
  675.3 15.4 %fusion.26 = f32[3072,384]{1,0:T(8,128)} fusion(f32[512,384]{1,0:T(8,128)S(1)} %get-tuple-element.761, f32[512,3072]{1,0:T(8,128)} %all-reduce.4.cloned.1.call-done, f32[512,3072]{1,0:T(8,128)} %all-gather.23.cloned.1.call-done, f32[512]{0:T(512)S(1)} %get-tuple-element.757, f32[512]{0:T(512)S(1)} %get-tuple-element.756), kind=kOutput, calls=%fused_computation.76 | convolution fusion | flops 7252475904 | bytes 18092032 | tf_op jit(solution)/shard_map/dot_general | solution.py:106
  690.7 2.1 constant_dynamic-slice_fusion.6
  692.8 10.5 %all-reduce = (f32[384]{0:T(512)}, f32[]{:T(128)}) all-reduce(f32[384]{0:T(512)S(1)} %get-tuple-element.760, f32[]{:T(128)} %get-tuple-element.744), channel_id=1, replica_groups=mesh['row'=4,'col'=8] {'row'}, use_global_device_ids=true, to_apply=%region_26.0 | all-reduce | flops 385 | bytes 3080 | tf_op jit(solution)/shard_map/psum | solution.py:114
  703.9 13.4 %reduce-scatter.5.cloned.1.call-done = f32[384,768]{1,0:T(8,128)} async-done(((f32[384,3072]{1,0:T(8,128)}), f32[384,768]{1,0:T(8,128)}) %reduce-scatter.5.cloned.1.call-update) | async-done | bytes 1179664 | tf_op jit(solution)/shard_map/reduce_scatter | solution.py:112
  717.3 60.4 %reduce-scatter.3.cloned.1.call-done = f32[768,384]{1,0:T(8,128)} async-done(((f32[3072,384]{1,0:T(8,128)}), f32[768,384]{1,0:T(8,128)}) %reduce-scatter.3.cloned.1.call-update) | async-done | bytes 1179664 | tf_op jit(solution)/shard_map/reduce_scatter | solution.py:111
  (111 shorter events, 1.8 us)
Async XLA Ops:
  7.2 69.9 %all-gather.23.cloned.1.call-start = ((), (), s32[]{:S(2)}) async-start(), calls=%async_computation.2 | async-start | bytes 7077888 | tf_op jit(solution)/shard_map/all_gather | solution.py:45
  7.9 165.9 %all-gather.25.cloned.1.call-start = ((), (), s32[]{:S(2)}) async-start(), calls=%async_computation.3 | async-start | bytes 11796480 | tf_op jit(solution)/shard_map/all_gather | solution.py:46
  8.6 464.9 %all-reduce.4.cloned.1.call-start = ((), (), s32[]{:S(2)}) async-start(), calls=%async_computation.4 | async-start | bytes 12582912 | tf_op jit(solution)/shard_map/psum | solution.py:75
  173.8 5.5 copy-start
  266.7 73.1 %copy-start.5 = (f32[512]{0:T(512)}, f32[512]{0:T(512)S(1)}, u32[]{:S(2)}) copy-start(f32[512]{0:T(512)S(1)} %add_subtract_fusion.2) | copy-start | bytes 6148
  293.9 45.8 %copy-start.4 = (f32[768]{0:T(1024)}, f32[768]{0:T(1024)S(1)}, u32[]{:S(2)}) copy-start(f32[768]{0:T(1024)S(1)} %add_subtract_fusion) | copy-start | bytes 9220
  339.8 0.7 copy-start.6
  339.8 133.8 %copy-start.7 = (f32[384]{0:T(512)S(1)}, f32[384]{0:T(512)}, u32[]{:S(2)}) copy-start(f32[384]{0:T(512)} %param.20) | copy-start | bytes 4612
  339.8 149.3 %slice-start = ((s8[4718592]{0:T(1024)(128)(4,1)}), s8[524288]{0:T(1024)(128)(4,1)S(1)}, s32[]{:S(2)}) async-start(s8[4718592]{0:T(1024)(128)(4,1)} %bitcast.67), calls=%async_computation.8 | async-start | bytes 1048576
  339.8 297.5 %all-reduce.6.cloned.1.call-start = ((), (), s32[]{:S(2)}) async-start(), calls=%async_computation.5 | async-start | bytes 12582912 | tf_op jit(solution)/shard_map/psum | solution.py:87
  473.6 15.5 %slice-start.1 = ((s8[4718592]{0:T(1024)(128)(4,1)}), s8[4194304]{0:T(1024)(128)(4,1)S(1)}, s32[]{:S(2)}) async-start(s8[4718592]{0:T(1024)(128)(4,1)} %bitcast.67), calls=%async_computation.9 | async-start | bytes 8388608
  488.2 0.9 copy-start.2
  501.1 216.2 %reduce-scatter.5.cloned.1.call-start = ((), (), s32[]{:S(2)}) async-start(), calls=%async_computation.7 | async-start | bytes 5898240 | tf_op jit(solution)/shard_map/reduce_scatter | solution.py:112
  646.8 2.6 copy-start.1
  660.1 1.1 copy-start.3
  660.1 117.6 %reduce-scatter.3.cloned.1.call-start = ((), (), s32[]{:S(2)}) async-start(), calls=%async_computation.6 | async-start | bytes 5898240 | tf_op jit(solution)/shard_map/reduce_scatter | solution.py:111
Sparse Core Ops, SparseCore 0:
  9.6 67.4 all-gather.22
  78.9 94.8 all-gather.24
  339.9 133.6 all-reduce.3
  501.2 136.0 all-reduce.5
  660.2 57.0 reduce-scatter.4
  720.7 56.9 reduce-scatter.2
where the time goes:
time: 794 us; the launch traced here: 786 us
  waiting for transfers between devices  506 us (64%)
  blocking collectives  129 us (16%)
  matrix products  104 us (13%)
  other arithmetic  20.5 us (3%)
  between operations  16.6 us (2%)
  local copies, waits for them, and re-layouts  8.41 us (1%)
    psum x1, waiting for transfers between devices, body(): out = lax.psum(part_out, 'col')  136 us
    psum x1, waiting for transfers between devices, body(): whole_targets = lax.psum(partial_value, 'col')  133 us
    all_gather x10, blocking collectives, merged(): everything = jax.tree.map(lambda part: lax.all_gather(part, axis), array)  118 us
    all_gather x1, waiting for transfers between devices, body(): full_images = lax.all_gather(images, 'row', axis=1, tiled=True)  93.5 us
    all_gather x1, waiting for transfers between devices, body(): full_noise = lax.all_gather(noise, 'col', axis=1, tiled=True)  68.3 us
    reduce_scatter x1, waiting for transfers between devices, body(): lax.psum_scatter(local_in, 'row', scatter_dimension=0, tiled=True)  60.4 us
    dot_general x1, matrix products, body(): jnp.dot(weights, full_images, precision=highest, preferred_element_type=j...  19.3 us
    dot_general x1, matrix products, body(): lax.dot_general(full_noise, full_images, (((1,), (1,)), ((), ())), precis...  18.3 us
  transfers between devices with their start and end apart: 6, of which 6 were waited for; matrix products, arithmetic and copies ran while one was open for 4% of the time, Pallas kernels for 0%

commit v1 on v0

--- a/solution.py
+++ b/solution.py
@@ -42,7 +42,10 @@
 
 def body(noise, images, time_index, w_in, time_gain, w_out):
     highest = lax.Precision.HIGHEST
-    full_noise = lax.all_gather(noise, "col", axis=1, tiled=True)
+    size = lax.axis_size("col")
+    blocks = jnp.stack([noise for _ in range(size)])
+    blocks = lax.all_to_all(blocks, "col", split_axis=0, concat_axis=0)
+    full_noise = jnp.concatenate(blocks, axis=1)
     full_images = lax.all_gather(images, "row", axis=1, tiled=True)
     width = full_noise.shape[1]
     noise_count = full_noise.shape[0] * lax.axis_size("row")

time: 794 us -> 778 us (0.980)
  waiting for transfers between devices: 506 us -> 483 us
  blocking collectives: 129 us -> 120 us
    all_to_all x0 -> x1, waiting for transfers between devices: none -> 139 us  [body(): blocks = lax.all_to_all(blocks, 'col', split_axis=0, concat_axis=0)]
    all_gather x1, waiting for transfers between devices: 93.5 us -> 0.02 us  [body(): full_images = lax.all_gather(images, 'row', axis=1, tiled=True)]
    all_gather x1 -> x0, waiting for transfers between devices: 68.3 us -> none  [body(): full_noise = lax.all_gather(noise, 'col', axis=1, tiled=True)]
    all_gather x10, blocking collectives: 118 us -> 109 us  [merged(): everything = jax.tree.map(lambda part: lax.all_gather(part, axis), array)]
  transfers between devices with their start and end apart: 6 -> 6, of which waited for: 6 -> 5; matrix products, arithmetic and copies ran while one was open for 4% -> 6% of each run, Pallas kernels for 0% -> 0%
where the time goes in v1:
time: 778 us; the launch traced here: 770 us
  waiting for transfers between devices  483 us (62%)
  blocking collectives  120 us (15%)
  matrix products  105 us (13%)
  other arithmetic  23.7 us (3%)
  between operations  16.3 us (2%)
  local copies, waits for them, and re-layouts  14.4 us (2%)
    all_to_all x1, waiting for transfers between devices, body(): blocks = lax.all_to_all(blocks, 'col', split_axis=0, concat_axis=0)  139 us
    psum x1, waiting for transfers between devices, body(): out = lax.psum(part_out, 'col')  136 us
    psum x1, waiting for transfers between devices, body(): whole_targets = lax.psum(partial_value, 'col')  133 us
    all_gather x10, blocking collectives, merged(): everything = jax.tree.map(lambda part: lax.all_gather(part, axis), array)  109 us
    reduce_scatter x1, waiting for transfers between devices, body(): lax.psum_scatter(local_in, 'row', scatter_dimension=0, tiled=True)  60.4 us
    dot_general x1, matrix products, body(): jnp.dot(weights, full_images, precision=highest, preferred_element_type=j...  19.3 us
    dot_general x1, matrix products, body(): lax.dot_general(full_noise, full_images, (((1,), (1,)), ((), ())), precis...  18.3 us
  transfers between devices with their start and end apart: 6, of which 5 were waited for; matrix products, arithmetic and copies ran while one was open for 6% of the time, Pallas kernels for 0%

profile of v1, /device:TPU:0, one launch (start us, length us, event | category | flops | bytes accessed | tf_op | source)
XLA Modules:
  0.0 769.9 jit_solution(1087133708891520876)
XLA Ops:
  7.2 0.7 all-gather.22.cloned.1.call-update
  7.9 4.2 stack.2
  12.1 6.4 all-to-all-start
  18.5 139.0 %all-to-all-done = f32[8,512,384]{2,1,0:T(8,128)} async-done(((f32[8,512,384]{2,1,0:T(8,128)}), f32[8,512,384]{2,1,0:T(8,128)}, u32[]{:S(2)}, u32[]{:S(2)}) %all-to-all-start) | async-done | bytes 6291488 | tf_op jit(solution)/shard_map/all_to_all | solution.py:47
  157.5 6.3 copy.24
  163.8 3.3 fusion
  167.1 4.5 multiply_reduce_fusion
  171.6 0.9 copy-done
  172.5 18.3 %subtract_reduce_fusion.3 = (f32[512]{0:T(512)S(1)}, f32[512,768]{1,0:T(8,128)S(1)}) fusion(f32[512,3072]{1,0:T(8,128)S(1)} %bitcast.76, f32[768,3072]{1,0:T(8,128)} %all-gather.22.cloned.1.call-done, f32[768]{0:T(1024)S(1)} %multiply_reduce_fusion, f32[512]{0:T(512)S(1)} %fusion), kind=kOutput, calls=%fused_computation.39 | convolution fusion | flops 14497873920 | bytes 17308672 | tf_op jit(solution)/shard_map/dot_general | solution.py:55
  190.8 0.4 exponential_reduce_fusion.4
  191.2 12.8 %all-gather.11 = f32[8,1,512]{2,1,0:T(1,128)S(1)} all-gather(f32[1,1,512]{2,1,0:T(1,128)S(1)} %bitcast.105), channel_id=3, replica_groups=mesh['row'=4,'col'=8] {'col'}, dimensions={0}, use_global_device_ids=true | all-gather | bytes 18432 | tf_op jit(solution)/shard_map/all_gather | solution.py:12
  204.0 12.8 %all-gather.10 = f32[8,1,512]{2,1,0:T(1,128)S(1)} all-gather(f32[1,1,512]{2,1,0:T(1,128)S(1)} %bitcast.103), channel_id=2, replica_groups=mesh['row'=4,'col'=8] {'col'}, dimensions={0}, use_global_device_ids=true | all-gather | bytes 18432 | tf_op jit(solution)/shard_map/all_gather | solution.py:12
  216.8 0.4 while.85
  217.4 0.3 exponential_reduce_fusion.3
  217.7 8.2 %all-gather.13 = f32[4,1,768]{2,1,0:T(1,128)S(1)} all-gather(f32[1,1,768]{2,1,0:T(1,128)S(1)} %reshape.75), channel_id=5, replica_groups=mesh['row'=4,'col'=8] {'row'}, dimensions={0}, use_global_device_ids=true | all-gather | bytes 15360 | tf_op jit(solution)/shard_map/all_gather | solution.py:12
  225.9 8.2 %all-gather.12 = f32[4,1,768]{2,1,0:T(1,128)S(1)} all-gather(f32[1,1,768]{2,1,0:T(1,128)S(1)} %reshape.73), channel_id=4, replica_groups=mesh['row'=4,'col'=8] {'row'}, dimensions={0}, use_global_device_ids=true | all-gather | bytes 15360 | tf_op jit(solution)/shard_map/all_gather | solution.py:12
  234.1 0.2 while.86
  234.4 0.2 subtract_reduce_fusion.1
  234.5 0.4 exponential_reduce_fusion.2
  235.0 12.8 %all-gather.15 = f32[8,1,512]{2,1,0:T(1,128)S(1)} all-gather(f32[1,1,512]{2,1,0:T(1,128)S(1)} %bitcast.104), channel_id=7, replica_groups=mesh['row'=4,'col'=8] {'col'}, dimensions={0}, use_global_device_ids=true | all-gather | bytes 18432 | tf_op jit(solution)/shard_map/all_gather | solution.py:12
  247.7 13.2 %all-gather.14 = f32[8,1,512]{2,1,0:T(1,128)S(1)} all-gather(f32[1,1,512]{2,1,0:T(1,128)S(1)} %bitcast.101), channel_id=6, replica_groups=mesh['row'=4,'col'=8] {'col'}, dimensions={0}, use_global_device_ids=true | all-gather | bytes 18432 | tf_op jit(solution)/shard_map/all_gather | solution.py:12
  261.0 0.4 while.87
  261.6 0.3 exponential_reduce_fusion.1
  261.9 7.2 all-gather.17
  269.2 8.2 %all-gather.16 = f32[4,1,768]{2,1,0:T(1,128)S(1)} all-gather(f32[1,1,768]{2,1,0:T(1,128)S(1)} %reshape.81), channel_id=8, replica_groups=mesh['row'=4,'col'=8] {'row'}, dimensions={0}, use_global_device_ids=true | all-gather | bytes 15360 | tf_op jit(solution)/shard_map/all_gather | solution.py:12
  277.3 0.2 while.88
  277.6 0.2 subtract_reduce_fusion.4
  277.8 0.4 exponential_reduce_fusion
  278.2 12.8 %all-gather.19 = f32[8,1,512]{2,1,0:T(1,128)S(1)} all-gather(f32[1,1,512]{2,1,0:T(1,128)S(1)} %bitcast.106), channel_id=11, replica_groups=mesh['row'=4,'col'=8] {'col'}, dimensions={0}, use_global_device_ids=true | all-gather | bytes 18432 | tf_op jit(solution)/shard_map/all_gather | solution.py:12
  291.0 12.8 %all-gather.18 = f32[8,1,512]{2,1,0:T(1,128)S(1)} all-gather(f32[1,1,512]{2,1,0:T(1,128)S(1)} %bitcast.102), channel_id=10, replica_groups=mesh['row'=4,'col'=8] {'col'}, dimensions={0}, use_global_device_ids=true | all-gather | bytes 18432 | tf_op jit(solution)/shard_map/all_gather | solution.py:12
  303.7 0.4 while.89
  304.1 19.3 %fusion.7 = f32[512,3072]{1,0:T(8,128)} fusion(f32[768,3072]{1,0:T(8,128)} %all-gather.22.cloned.1.call-done, f32[512,768]{1,0:T(8,128)S(1)} %get-tuple-element.759, f32[512]{0:T(512)S(1)} %log_add_fusion, f32[768]{0:T(1024)S(1)} %add_subtract_fusion), kind=kOutput, calls=%fused_computation.27 | convolution fusion | flops 14496301056 | bytes 17306624 | tf_op jit(solution)/shard_map/dot_general | solution.py:73
  323.4 0.2 all-reduce.6.cloned.1.call-start
  323.7 0.4 copy-done.3
  324.1 133.1 %all-reduce.4.cloned.1.call-done = f32[512,3072]{1,0:T(8,128)} async-done(((f32[512,3072]{1,0:T(8,128)}), f32[512,3072]{1,0:T(8,128)}) %all-reduce.4.cloned.1.call-update) | async-done | bytes 6291472 | tf_op jit(solution)/shard_map/psum | solution.py:78
  457.2 14.5 %convolution_add_fusion = f32[512,384]{1,0:T(8,128)S(1)} fusion(f32[3072,384]{1,0:T(8,128)} %param.19, f32[384]{0:T(512)S(1)} %copy-done.4, f32[512]{0:T(512)S(1)} %get-tuple-element.757, f32[512,3072]{1,0:T(8,128)} %all-reduce.4.cloned.1.call-done, f32[512,3072]{1,0:T(8,128)} %bitcast.73, f32[512]{0:T(512)S(1)} %get-tuple-element.756), kind=kOutput, calls=%fused_computation.44 | convolution fusion | flops 7252869120 | bytes 18093568 | tf_op jit(solution)/shard_map/dot_general | solution.py:84
  471.8 12.0 %fusion.21 = f32[512,3072]{1,0:T(8,128)} fusion(f32[384,3072]{1,0:T(8,128)S(1)} %bitcast.78, f32[512,384]{1,0:T(8,128)S(1)} %convolution_add_fusion), kind=kOutput, calls=%fused_computation.50 | convolution fusion | flops 7248543744 | bytes 11796480 | tf_op jit(solution)/shard_map/dot_general | solution.py:89
  483.8 0.3 reduce-scatter.5.cloned.1.call-start
  484.1 136.0 %all-reduce.6.cloned.1.call-done = f32[512,3072]{1,0:T(8,128)} async-done(((f32[512,3072]{1,0:T(8,128)}), f32[512,3072]{1,0:T(8,128)}) %all-reduce.6.cloned.1.call-update) | async-done | bytes 6291472 | tf_op jit(solution)/shard_map/psum | solution.py:90
  620.1 12.7 %multiply_reduce_fusion.1 = (f32[]{:T(128)}, f32[512,3072]{1,0:T(8,128)}) fusion(f32[512,3072]{1,0:T(8,128)} %all-reduce.6.cloned.1.call-done, f32[512,3072]{1,0:T(8,128)} %all-reduce.4.cloned.1.call-done, f32[512,3072]{1,0:T(8,128)} %bitcast.74), kind=kLoop, calls=%fused_computation.18 | loop fusion | flops 6291455 | bytes 25165828 | tf_op jit(solution)/shard_map/reduce_sum | solution.py:92
  632.8 11.3 %fusion.1 = f32[384,3072]{1,0:T(8,128)} fusion(f32[512,3072]{1,0:T(8,128)} %get-tuple-element.745, f32[512,384]{1,0:T(8,128)S(1)} %convolution_add_fusion), kind=kOutput, calls=%fused_computation.21 | convolution fusion | flops 7250116608 | bytes 11796480 | tf_op jit(solution)/shard_map/dot_general | solution.py:94
  644.1 0.3 reduce-scatter.3.cloned.1.call-start
  644.4 14.1 %multiply_reduce_fusion.2 = (f32[384]{0:T(512)S(1)}, f32[512,384]{1,0:T(8,128)S(1)}) fusion(f32[512]{0:T(512)S(1)} %get-tuple-element.757, f32[512,384]{1,0:T(8,128)S(1)} %convolution_add_fusion, f32[384,3072]{1,0:T(8,128)} %param.21, f32[512,3072]{1,0:T(8,128)} %get-tuple-element.745), kind=kOutput, calls=%fused_computation.45 | convolution fusion | flops 7251295744 | bytes 12586496 | tf_op jit(solution)/shard_map/dot_general | solution.py:101
  658.5 15.2 %fusion.27 = f32[3072,384]{1,0:T(8,128)} fusion(f32[512,384]{1,0:T(8,128)S(1)} %get-tuple-element.761, f32[512,3072]{1,0:T(8,128)} %all-reduce.4.cloned.1.call-done, f32[512,3072]{1,0:T(8,128)} %bitcast.75, f32[512]{0:T(512)S(1)} %get-tuple-element.757, f32[512]{0:T(512)S(1)} %get-tuple-element.756), kind=kOutput, calls=%fused_computation.77 | convolution fusion | flops 7252475904 | bytes 18092032 | tf_op jit(solution)/shard_map/dot_general | solution.py:109
  673.7 2.1 constant_dynamic-slice_fusion.6
  675.8 10.8 %all-reduce = (f32[384]{0:T(512)}, f32[]{:T(128)}) all-reduce(f32[384]{0:T(512)S(1)} %get-tuple-element.760, f32[]{:T(128)} %get-tuple-element.744), channel_id=1, replica_groups=mesh['row'=4,'col'=8] {'row'}, use_global_device_ids=true, to_apply=%region_26.0 | all-reduce | flops 385 | bytes 3080 | tf_op jit(solution)/shard_map/psum | solution.py:117
  687.2 14.2 %reduce-scatter.5.cloned.1.call-done = f32[384,768]{1,0:T(8,128)} async-done(((f32[384,3072]{1,0:T(8,128)}), f32[384,768]{1,0:T(8,128)}) %reduce-scatter.5.cloned.1.call-update) | async-done | bytes 1179664 | tf_op jit(solution)/shard_map/reduce_scatter | solution.py:115
  701.3 60.4 %reduce-scatter.3.cloned.1.call-done = f32[768,384]{1,0:T(8,128)} async-done(((f32[3072,384]{1,0:T(8,128)}), f32[768,384]{1,0:T(8,128)}) %reduce-scatter.3.cloned.1.call-update) | async-done | bytes 1179664 | tf_op jit(solution)/shard_map/reduce_scatter | solution.py:114
  (106 shorter events, 1.6 us)
Async XLA Ops:
  7.2 159.9 %all-gather.22.cloned.1.call-start = ((), (), s32[]{:S(2)}) async-start(), calls=%async_computation.3 | async-start | bytes 11796480 | tf_op jit(solution)/shard_map/all_gather | solution.py:49
  12.1 145.4 %all-to-all-start = ((f32[8,512,384]{2,1,0:T(8,128)}), f32[8,512,384]{2,1,0:T(8,128)}, u32[]{:S(2)}, u32[]{:S(2)}) async-start(f32[8,512,384]{2,1,0:T(8,128)} %stack.2), calls=%async_computation | async-start | bytes 12582912 | tf_op jit(solution)/shard_map/all_to_all | solution.py:47
  18.5 438.8 %all-reduce.4.cloned.1.call-start = ((), (), s32[]{:S(2)}) async-start(), calls=%async_computation.4 | async-start | bytes 12582912 | tf_op jit(solution)/shard_map/psum | solution.py:78
  167.1 5.5 copy-start
  261.4 62.0 %copy-start.2 = (f32[512]{0:T(512)}, f32[512]{0:T(512)S(1)}, u32[]{:S(2)}) copy-start(f32[512]{0:T(512)S(1)} %add_subtract_fusion.2) | copy-start | bytes 6148
  277.6 45.8 %copy-start.1 = (f32[768]{0:T(1024)}, f32[768]{0:T(1024)S(1)}, u32[]{:S(2)}) copy-start(f32[768]{0:T(1024)S(1)} %add_subtract_fusion) | copy-start | bytes 9220
  323.4 0.7 copy-start.3
  323.4 133.8 %copy-start.4 = (f32[384]{0:T(512)S(1)}, f32[384]{0:T(512)}, u32[]{:S(2)}) copy-start(f32[384]{0:T(512)} %param.20) | copy-start | bytes 4612
  323.4 148.4 %slice-start = ((s8[4718592]{0:T(1024)(128)(4,1)}), s8[524288]{0:T(1024)(128)(4,1)S(1)}, s32[]{:S(2)}) async-start(s8[4718592]{0:T(1024)(128)(4,1)} %bitcast.77), calls=%async_computation.8 | async-start | bytes 1048576
  323.4 296.6 %all-reduce.6.cloned.1.call-start = ((), (), s32[]{:S(2)}) async-start(), calls=%async_computation.5 | async-start | bytes 12582912 | tf_op jit(solution)/shard_map/psum | solution.py:90
  457.2 14.5 %slice-start.1 = ((s8[4718592]{0:T(1024)(128)(4,1)}), s8[4194304]{0:T(1024)(128)(4,1)S(1)}, s32[]{:S(2)}) async-start(s8[4718592]{0:T(1024)(128)(4,1)} %bitcast.77), calls=%async_computation.9 | async-start | bytes 8388608
  483.8 217.5 %reduce-scatter.5.cloned.1.call-start = ((), (), s32[]{:S(2)}) async-start(), calls=%async_computation.7 | async-start | bytes 5898240 | tf_op jit(solution)/shard_map/reduce_scatter | solution.py:115
  644.1 117.6 %reduce-scatter.3.cloned.1.call-start = ((), (), s32[]{:S(2)}) async-start(), calls=%async_computation.6 | async-start | bytes 5898240 | tf_op jit(solution)/shard_map/reduce_scatter | solution.py:114
Sparse Core Ops, SparseCore 0:
  9.8 98.9 all-gather.21
  323.6 133.6 all-reduce.3
  484.0 136.0 all-reduce.5
  644.3 57.0 reduce-scatter.4
  704.7 56.9 reduce-scatter.2
